TPU v7x, 32 devices: a whole 2x2x4 slice. The times are simulated.
32 devices in a mesh: stat: 16 (over z, x, core), tm: 2 (over y).
Axes of the slice: x: 2, y: 2, z: 4, core: 2. Of those that a mesh axis runs over, the one named last changes fastest.
Arguments:
- voltages: bfloat16 [2, 1024, 8, 4096], P(None, 'stat', 'tm'), may hold values from -6 to 6
- beam_weights: bfloat16 [2, 1024, 256], P(None, 'stat'), may hold values from -0.125 to 0.125
Outputs:
- beams: bfloat16 [4096, 8, 2, 256], P('stat', 'tm')
- visibilities: float32 [1024, 32, 2, 1024], P('tm', 'stat')
All inputs are finite; a program needn't handle non-finite values.
Results may differ from a plain program's by a relative error of at most 0.011.
Values may be sent and summed in bfloat16 or wider, within the bound.
A program may use at most 64 MiB of HBM per device.

v0:
```python
import math

import jax
import jax.numpy as jnp
from jax import lax
from jax.sharding import PartitionSpec as P

INPUTS = 1024
NA = 16
NB = 256
BEAMS = 256
AVG = 128


def dft_block(length):
    index = jnp.arange(length, dtype=jnp.int32)
    product = index[:, None] * index[None, :] % length
    angle = product.astype(jnp.float32) * (2.0 * math.pi / length)
    cosine = jnp.cos(angle)
    sine = jnp.sin(angle)
    return jnp.stack([jnp.stack([cosine, -sine]), jnp.stack([sine, cosine])])


def fine_spectra(voltages):
    block_inputs = voltages.shape[1]
    spectra_count = voltages.shape[2]
    signal = voltages.astype(jnp.float32).reshape(2, block_inputs, spectra_count, NA, NB)
    first = jnp.einsum("poak,pisab->osikb", dft_block(NA), signal, precision=lax.Precision.HIGH)
    outer_index = jnp.arange(NA, dtype=jnp.int32)
    inner_index = jnp.arange(NB, dtype=jnp.int32)
    rotation = (outer_index[:, None] * inner_index[None, :] % (NA * NB)).astype(jnp.float32) * (
        2.0 * math.pi / (NA * NB)
    )
    cos_twist = jnp.cos(rotation)
    sin_twist = jnp.sin(rotation)
    rotated = jnp.stack(
        [first[0] * cos_twist + first[1] * sin_twist, first[1] * cos_twist - first[0] * sin_twist]
    )
    final = jnp.einsum("osikb,ocbq->csiqk", rotated, dft_block(NB), precision=lax.Precision.HIGH)
    norm_factor = 1.0 / math.sqrt(NA * NB)
    return (
        (final * norm_factor).reshape(2, spectra_count, block_inputs, NA * NB).astype(jnp.bfloat16)
    )


def stack_weights(weights):
    return jnp.stack(
        [jnp.stack([weights[0], weights[1]], 1), jnp.stack([-weights[1], weights[0]], 1)], 0
    )


def body(voltages, beam_weights):
    stat_count = lax.axis_size("stat")
    time_count = lax.axis_size("tm")
    block_inputs = voltages.shape[1]
    spectra = fine_spectra(voltages)
    spectra_count = spectra.shape[1]
    channel_share = NA * NB // stat_count
    all_weights = lax.all_gather(beam_weights, "stat", axis=1, tiled=True)
    full_stack = stack_weights(all_weights)
    turned = lax.all_to_all(spectra, "stat", split_axis=3, concat_axis=2, tiled=True)
    item_count = turned.shape[1]

    def add_block(block_index, running):
        offset = (block_index * block_inputs).astype(jnp.int32)
        spec_block = lax.dynamic_slice_in_dim(turned, offset, block_inputs, 2)
        weight_block = lax.dynamic_slice_in_dim(full_stack, offset, block_inputs, 1)
        partial_value = jnp.einsum(
            "psic,piqb->csqb", spec_block, weight_block, preferred_element_type=jnp.float32
        )
        rounded = lax.optimization_barrier(partial_value.astype(jnp.bfloat16))
        return running + rounded.astype(jnp.float32)

    initial = jnp.zeros((turned.shape[3], item_count, 2, BEAMS), jnp.float32)
    beams = lax.fori_loop(0, stat_count, add_block, initial).astype(jnp.bfloat16)
    local_vch = channel_share // AVG
    scale = 1.0 / (spectra_count * time_count * AVG)
    split = turned.reshape(2, spectra_count, INPUTS, local_vch, AVG)
    real_gram = jnp.einsum("psiva,psjva->ivj", split, split, preferred_element_type=jnp.float32)
    mixed = jnp.einsum("siva,sjva->ivj", split[1], split[0], preferred_element_type=jnp.float32)
    mixed = mixed - jnp.einsum(
        "siva,sjva->ivj", split[0], split[1], preferred_element_type=jnp.float32
    )
    visibilities = lax.psum_scatter(
        (jnp.stack([real_gram, mixed], axis=2) * scale).astype(jnp.bfloat16),
        "tm",
        scatter_dimension=0,
        tiled=True,
    ).astype(jnp.float32)
    return (beams, visibilities)


def solution(mesh):
    return jax.shard_map(
        body,
        mesh=mesh,
        in_specs=(P(None, "stat", "tm", None), P(None, "stat", None)),
        out_specs=(P("stat", "tm", None, None), P("tm", "stat", None, None)),
        check_vma=False,
    )
```

profile of v0, /device:TPU:0, one launch (start us, length us, event | category | flops | bytes accessed | tf_op | source)
XLA Modules:
  0.0 378.3 jit_solution(18396577974899452304)
XLA Ops:
  10.2 7.7 %reshape.219 = bf16[2,64,4,16,256]{4,3,2,1,0:T(8,128)(2,1)} reshape(bf16[2,64,4,4096]{3,2,1,0:T(4,128)(2,1)} %param.4) | data formatting | bytes 8388608 | tf_op jit(solution)/shard_map/reshape | solution.py:27
  17.9 4.6 %fusion.21 = f32[2,4,64,16,256]{4,3,1,2,0:T(8,128)S(1)} fusion(bf16[2,64,4,16,256]{4,3,2,1,0:T(8,128)(2,1)} %reshape.219, f32[1,2,16,16]{2,3,0,1:T(8,128)S(1)} %get-tuple-element.132, f32[1,2,16,16]{2,3,0,1:T(8,128)S(1)} %get-tuple-element.131), kind=kOutput, calls=%fused_computation.27 | convolution fusion | flops 402654208 | bytes 12587008 | tf_op jit(solution)/shard_map/poak,pisab->osikb/dot_general | solution.py:28
  26.5 11.1 %fusion.12 = bf16[2,4,64,256,16]{3,2,4,1,0:T(8,128)(2,1)} fusion(f32[2,4,64,16,256]{4,3,1,2,0:T(8,128)S(1)} %pad_maximum_fusion, f32[1,2,256,256]{3,2,0,1:T(8,128)S(1)} %get-tuple-element.130, f32[1,2,256,256]{3,2,0,1:T(8,128)S(1)} %get-tuple-element.129), kind=kOutput, calls=%fused_computation.18 | convolution fusion | flops 6446907392 | bytes 13631488 | tf_op jit(solution)/shard_map/osikb,ocbq->csiqk/dot_general | solution.py:39
  37.6 10.9 %copy.54 = bf16[2,4,64,256,16]{2,4,3,1,0:T(8,128)(2,1)} copy(bf16[2,4,64,256,16]{3,2,4,1,0:T(8,128)(2,1)} %fusion.12) | data formatting | bytes 8388608 | tf_op jit(solution)/shard_map/convert_element_type | solution.py:42
  48.5 12.2 %copy.108 = bf16[2,4,64,4096]{2,1,0,3:T(4,128)(2,1)} copy(bf16[2,4,64,4096]{2,3,1,0:T(8,128)(2,1)} %bitcast.121) | data formatting | bytes 8388608 | tf_op jit(solution)/shard_map/convert_element_type | solution.py:42
  60.7 14.0 %reshape.233 = bf16[16,2,65536]{2,1,0:T(2,128)(2,1)} reshape(bf16[4096,2,4,64]{3,2,1,0:T(4,128)(2,1)} %bitcast.122) | data formatting | bytes 8388608
  74.7 7.4 %all-to-all-start = ((bf16[16,2,65536]{2,1,0:T(2,128)(2,1)}), bf16[16,2,65536]{2,1,0:T(2,128)(2,1)}, u32[]{:S(2)}, u32[]{:S(2)}) async-start(bf16[16,2,65536]{2,1,0:T(2,128)(2,1)} %reshape.233), calls=%async_computation | async-start | bytes 8388608 | tf_op jit(solution)/shard_map/all_to_all | solution.py:61
  82.9 83.0 %all-to-all-done = bf16[16,2,65536]{2,1,0:T(2,128)(2,1)} async-done(((bf16[16,2,65536]{2,1,0:T(2,128)(2,1)}), bf16[16,2,65536]{2,1,0:T(2,128)(2,1)}, u32[]{:S(2)}, u32[]{:S(2)}) %all-to-all-start) | async-done | bytes 4194336 | tf_op jit(solution)/shard_map/all_to_all | solution.py:61
  165.9 13.6 %reshape.234 = bf16[4096,2,4,64]{3,2,1,0:T(4,128)(2,1)} reshape(bf16[16,2,65536]{2,1,0:T(2,128)(2,1)} %all-to-all-done) | data formatting | bytes 8388608
  179.5 10.1 %copy.79 = bf16[2,4,64,16,256]{4,3,2,1,0:T(8,128)(2,1)} copy(bf16[2,4,64,16,256]{2,1,0,4,3:T(4,128)(2,1)} %bitcast.118) | data formatting | bytes 8388608 | tf_op jit(solution)/shard_map/all_to_all | solution.py:61
  189.6 12.7 %copy.82 = bf16[2,4,64,16,256]{4,2,3,1,0:T(8,128)(2,1)} copy(bf16[2,4,64,16,256]{2,1,0,4,3:T(4,128)(2,1)} %bitcast.119) | data formatting | bytes 8388608 | tf_op jit(solution)/shard_map/all_to_all | solution.py:61
  202.3 3.9 %fusion.64 = (bf16[1,4,16,64,256]{4,2,3,1,0:T(8,128)(2,1)}, bf16[1,4,16,64,256]{4,2,3,1,0:T(8,128)(2,1)S(1)}) fusion(bf16[2,4,16,64,256]{4,2,3,1,0:T(8,128)(2,1)} %bitcast.124), kind=kLoop, calls=%fused_computation.86 | loop fusion | bytes 8388608 | tf_op jit(solution)/shard_map/slice | solution.py:80
  208.4 2.5 squeeze.5
  210.9 3.7 copy.63
  214.6 4.0 %squeeze.4 = bf16[4,1024,2,128]{3,2,1,0:T(2,128)(2,1)} reshape(bf16[1,4,16,64,256]{4,3,2,1,0:T(8,128)(2,1)} %copy.63) | data formatting | bytes 4194304 | tf_op jit(solution)/shard_map/squeeze | solution.py:80
  218.7 7.0 %reshape.220 = bf16[2,4,1024,2,128]{4,3,2,1,0:T(2,128)(2,1)} reshape(bf16[2,4,16,64,256]{4,3,2,1,0:T(8,128)(2,1)} %bitcast.123) | data formatting | bytes 8388608 | tf_op jit(solution)/shard_map/reshape | solution.py:78
  225.6 4.1 %fusion.27 = f32[2,1024,1024,1]{2,1,3,0:T(8,128)S(1)} fusion(bf16[4,1024,2,128]{3,2,1,0:T(2,128)(2,1)S(1)} %squeeze.5, bf16[4,1024,2,128]{3,2,1,0:T(2,128)(2,1)} %squeeze.4), kind=kOutput, calls=%fused_computation.30 | convolution fusion | flops 2147483648 | bytes 12582912 | tf_op jit(solution)/shard_map/siva,sjva->ivj/dot_general | solution.py:80
  229.8 2.5 fusion.7
  232.2 7.8 %fusion.18 = f32[1024,2,1,1024]{0,3,1,2:T(8,128)S(1)} fusion(bf16[2,4,1024,2,128]{4,3,2,1,0:T(2,128)(2,1)} %reshape.220), kind=kOutput, calls=%fused_computation.26 | convolution fusion | flops 4294967296 | bytes 12582912 | tf_op jit(solution)/shard_map/psiva,psjva->ivj/dot_general | solution.py:79
  240.1 4.6 %fusion.6 = bf16[1024,2,2,1024]{0,3,1,2:T(8,128)(2,1)} fusion(f32[1024,2,1,1024]{0,3,1,2:T(8,128)S(1)} %fusion.7, f32[1024,2,1,1024]{0,3,1,2:T(8,128)S(1)} %fusion.18), kind=kLoop, calls=%fused_computation.9 | loop fusion | flops 12582912 | bytes 25165824 | tf_op jit(solution)/shard_map/convert_element_type | solution.py:85
  248.8 12.7 %copy.81 = bf16[2,4,64,16,256]{4,2,3,0,1:T(8,128)(2,1)} copy(bf16[2,4,64,16,256]{2,1,0,4,3:T(4,128)(2,1)} %bitcast.120) | data formatting | bytes 8388608 | tf_op jit(solution)/shard_map/all_to_all | solution.py:61
  261.5 35.2 %while.14 = (s32[]{:T(128)}, f32[256,4,2,256]{0,3,1,2:T(8,128)S(1)}, bf16[2,1024,2,256]{3,1,0,2:T(8,128)(2,1)}, bf16[2,4,1024,256]{3,2,0,1:T(8,128)(2,1)}, s32[]{:T(128)}, /*index=5*/s32[]{:T(128)}, s32[]{:T(128)}, s32[]{:T(128)}) while((s32[]{:T(128)}, f32[256,4,2,256]{0,3,1,2:T(8,128)S(1)}, bf16[2,1024,2,256]{3,1,0,2:T(8,128)(2,1)}, ...), condition=%wide.region_1.2_spmd.clone, body=%wide.region_0.1_spmd.clone.sunk | while | flops 136314880 | bytes 6685845 | solution.py:75
  298.9 60.1 %reduce-scatter.2.cloned.1.call-done = bf16[512,2,2,1024]{0,3,1,2:T(8,128)(2,1)} async-done(((bf16[1024,2,2,1024]{0,3,1,2:T(8,128)(2,1)}), bf16[512,2,2,1024]{0,3,1,2:T(8,128)(2,1)}) %reduce-scatter.2.cloned.1.call-update) | async-done | bytes 4194320 | tf_op jit(solution)/shard_map/reduce_scatter | solution.py:84
  359.1 11.8 %copy.69 = f32[512,2,2,1024]{3,2,1,0:T(2,128)} copy(bf16[512,2,2,1024]{0,3,1,2:T(8,128)(2,1)} %reduce-scatter.2.cloned.1.call-done) | data formatting | bytes 12582912
  (55 shorter events, 50.1 us)
Async XLA Ops:
  74.7 91.3 %all-to-all-start = ((bf16[16,2,65536]{2,1,0:T(2,128)(2,1)}), bf16[16,2,65536]{2,1,0:T(2,128)(2,1)}, u32[]{:S(2)}, u32[]{:S(2)}) async-start(bf16[16,2,65536]{2,1,0:T(2,128)(2,1)} %reshape.233), calls=%async_computation | async-start | bytes 8388608 | tf_op jit(solution)/shard_map/all_to_all | solution.py:61
  82.1 162.6 %all-gather.2.cloned.1.call-start = ((), (), s32[]{:S(2)}) async-start(), calls=%async_computation.2 | async-start | bytes 1114112 | tf_op jit(solution)/shard_map/all_gather | solution.py:59
  82.8 276.2 %reduce-scatter.2.cloned.1.call-start = ((), (), s32[]{:S(2)}) async-start(), calls=%async_computation.3 | async-start | bytes 12582912 | tf_op jit(solution)/shard_map/reduce_scatter | solution.py:84
  225.6 4.1 %copy-start = (bf16[4,1024,2,128]{3,2,1,0:T(2,128)(2,1)S(1)}, bf16[4,1024,2,128]{3,2,1,0:T(2,128)(2,1)}, u32[]{:S(2)}) copy-start(bf16[4,1024,2,128]{3,2,1,0:T(2,128)(2,1)} %squeeze.4) | copy-start | bytes 6291460
Sparse Core Ops, SparseCore 0:
  85.1 74.9 all-gather.1
Sparse Core Ops, SparseCore 1:
  244.8 114.3 reduce-scatter.1
where the time goes:
time: 381 us; the launch traced here: 378 us
  waiting for transfers between devices  144 us (38%)
  local copies, waits for them, and re-layouts  132 us (35%)
  matrix products  54 us (14%)
  other arithmetic  24.3 us (6%)
  between operations  15.6 us (4%)
  starting transfers between devices  7.51 us (2%)
    all_to_all x1, waiting for transfers between devices, body(): lax.all_to_all(spectra, 'stat', split_axis=3, concat_axis=2, tiled=True)  83 us
    reduce_scatter x1, waiting for transfers between devices, body(): lax.psum_scatter((jnp.stack([real_gram, mixed], axis=2) * scale).astype(j...  60.1 us
    unnamed x5, local copies, waits for them, and re-layouts  39.4 us
    all_to_all x3, local copies, waits for them, and re-layouts, body(): lax.all_to_all(spectra, 'stat', split_axis=3, concat_axis=2, tiled=True)  35.5 us
    dot_general x16, matrix products, add_block(): jnp.einsum('psic,piqb->csqb', spec_block, weight_block, preferred_element...  23.9 us
    convert_element_type x2, local copies, waits for them, and re-layouts, fine_spectra(): (final * norm_factor).reshape(2, spectra_count, block_inputs, NA * NB)  23.1 us
    dot_general x1, matrix products, fine_spectra(): jnp.einsum('osikb,ocbq->csiqk', rotated, dft_block(NB), precision=lax.Pre...  11.1 us
    add x16, other arithmetic, add_block(): return running + rounded.astype(jnp.float32)  10.8 us
  transfers between devices with their start and end apart: 3, of which 2 were waited for; matrix products, arithmetic and copies ran while one was open for 35% of the time, Pallas kernels for 0%

commit v1 on v0

--- a/solution.py
+++ b/solution.py
@@ -1,14 +1,16 @@
+import functools
 import math
 
 import jax
 import jax.numpy as jnp
+import numpy as np
 from jax import lax
+from jax.experimental import pallas as pl
+from jax.experimental.pallas import tpu as pltpu
 from jax.sharding import PartitionSpec as P
 
-INPUTS = 1024
 NA = 16
 NB = 256
-BEAMS = 256
 AVG = 128
 
 
@@ -71,11 +73,11 @@
         rounded = lax.optimization_barrier(partial_value.astype(jnp.bfloat16))
         return running + rounded.astype(jnp.float32)
 
-    initial = jnp.zeros((turned.shape[3], item_count, 2, BEAMS), jnp.float32)
+    initial = jnp.zeros((turned.shape[3], item_count, 2, beam_weights.shape[2]), jnp.float32)
     beams = lax.fori_loop(0, stat_count, add_block, initial).astype(jnp.bfloat16)
     local_vch = channel_share // AVG
     scale = 1.0 / (spectra_count * time_count * AVG)
-    split = turned.reshape(2, spectra_count, INPUTS, local_vch, AVG)
+    split = turned.reshape(2, spectra_count, stat_count * block_inputs, local_vch, AVG)
     real_gram = jnp.einsum("psiva,psjva->ivj", split, split, preferred_element_type=jnp.float32)
     mixed = jnp.einsum("siva,sjva->ivj", split[1], split[0], preferred_element_type=jnp.float32)
     mixed = mixed - jnp.einsum(
@@ -89,12 +91,310 @@
     ).astype(jnp.float32)
     return (beams, visibilities)
 
+RADIX = 8
+
+
+def dft_tables(points):
+    inner = points // RADIX
+    index = np.arange(inner)
+    angle = 2.0 * np.pi * (index[:, None] * index[None, :] % inner) / inner
+    scale = 1.0 / math.sqrt(points)
+    matrix = np.concatenate([np.cos(angle), np.sin(angle)], 1) * scale
+    turn = 2.0 * np.pi * (np.arange(RADIX)[:, None] * index[None, :]) / points
+    return (
+        jnp.asarray(matrix, jnp.bfloat16),
+        jnp.asarray(np.cos(turn), jnp.float32),
+        jnp.asarray(np.sin(turn), jnp.float32),
+    )
+
+
+def cadd(a, b):
+    return a[0] + b[0], a[1] + b[1]
+
+
+def csub(a, b):
+    return a[0] - b[0], a[1] - b[1]
+
+
+def times_minus_i(a):
+    return a[1], -a[0]
+
+
+def radix4(a):
+    s02, d02 = cadd(a[0], a[2]), csub(a[0], a[2])
+    s13, d13 = cadd(a[1], a[3]), times_minus_i(csub(a[1], a[3]))
+    return [cadd(s02, s13), cadd(d02, d13), csub(s02, s13), csub(d02, d13)]
+
+
+def radix8(a):
+    even, odd = radix4(a[0::2]), radix4(a[1::2])
+    root = math.sqrt(0.5)
+    o1, o2, o3 = odd[1], times_minus_i(odd[2]), odd[3]
+    o1 = ((o1[0] + o1[1]) * root, (o1[1] - o1[0]) * root)
+    o3 = ((o3[1] - o3[0]) * root, (-o3[0] - o3[1]) * root)
+    odd = [odd[0], o1, o2, o3]
+    return [cadd(e, o) for e, o in zip(even, odd)] + [csub(e, o) for e, o in zip(even, odd)]
+
+
+def fft_kernel(x_ref, m_ref, cos_ref, sin_ref, out_ref, mid):
+    rows, points = x_ref.shape[2:]
+    inner = points // RADIX
+    chunk = 16
+
+    @pl.loop(0, rows // chunk)
+    def _(step):
+        at = pl.ds(pl.multiple_of(step * chunk, chunk), chunk)
+        low = pl.ds(pl.multiple_of(rows + step * chunk, chunk), chunk)
+        for lane in range(0, inner, 128):
+            parts = []
+            for n1 in range(RADIX):
+                cut = pl.ds(n1 * inner + lane, 128)
+                parts.append(
+                    (x_ref[0, 0, at, cut].astype(jnp.float32), x_ref[1, 0, at, cut].astype(jnp.float32))
+                )
+            for k1, (re, im) in enumerate(radix8(parts)):
+                if k1:
+                    c, s = cos_ref[k1:k1 + 1, lane:lane + 128], sin_ref[k1:k1 + 1, lane:lane + 128]
+                    re, im = re * c + im * s, im * c - re * s
+                re, im = re.astype(jnp.bfloat16), im.astype(jnp.bfloat16)
+                left, right = pl.ds(lane, 128), pl.ds(inner + lane, 128)
+                mid[k1, at, left] = re
+                mid[k1, at, right] = im
+                mid[k1, low, left] = im
+                mid[k1, low, right] = -re
+
+    width = 2 * rows
+    for k1 in range(0, RADIX, 2):
+        pair = mid[k1:k1 + 2].reshape(2 * width, 2 * inner)
+        done = lax.dot_general(
+            m_ref[...], pair, (((1,), (1,)), ((), ())), preferred_element_type=jnp.float32
+        ).astype(jnp.bfloat16)
+        for half in range(2):
+            out_ref[:, :, 0, k1 + half] = done[:, half * width:(half + 1) * width].reshape(
+                out_ref.shape[0], out_ref.shape[1], out_ref.shape[4], width
+            )
+
+
+def spectra_blocks(voltages, stat_count, local_vch):
+    _, rows, items, points = voltages.shape
+    inner = points // RADIX
+    fine = AVG // RADIX
+    matrix, cos_turn, sin_turn = dft_tables(points)
+    whole = lambda shape: pl.BlockSpec(shape, lambda s: (0,) * len(shape))
+    return pl.pallas_call(
+        fft_kernel,
+        grid=(items,),
+        in_specs=[
+            pl.BlockSpec((2, 1, rows, points), lambda s: (0, s, 0, 0)),
+            whole(matrix.shape),
+            whole(cos_turn.shape),
+            whole(sin_turn.shape),
+        ],
+        out_specs=pl.BlockSpec(
+            (stat_count, local_vch, 1, RADIX, fine, 2 * rows), lambda s: (0, 0, s, 0, 0, 0)
+        ),
+        out_shape=jax.ShapeDtypeStruct(
+            (stat_count, local_vch, items, RADIX, fine, 2 * rows), jnp.bfloat16
+        ),
+        scratch_shapes=[pltpu.VMEM((RADIX, 2 * rows, 2 * inner), jnp.bfloat16)],
+        name="fft",
+    )(voltages.transpose(0, 2, 1, 3), matrix, cos_turn, sin_turn)
+
+
+def exchange_kernel(stat_count, time_count, spec_ref, w_ref, y_ref, wg_ref, own, wown, loc, wloc,
+                    send, recv, wsend, wrecv, fsend, frecv):
+    me, now = lax.axis_index("stat"), lax.axis_index("tm")
+    width = spec_ref.shape[-1]
+
+    def place(time, source):
+        return y_ref.at[:, time, :, pl.ds(pl.multiple_of(source * width, width), width)]
+
+    def forward(source, src, k):
+        made = []
+        for j in range(1, time_count):
+            copy = pltpu.make_async_remote_copy(
+                src_ref=src, dst_ref=place(now, source),
+                send_sem=fsend.at[j, k], recv_sem=frecv.at[j, k],
+                device_id={"tm": lax.rem(now + j, time_count)}, device_id_type=pl.DeviceIdType.MESH)
+            copy.start()
+            made.append(copy)
+        return made
+
+    barrier = pltpu.get_barrier_semaphore()
+    for k in range(1, stat_count):
+        pl.semaphore_signal(barrier, inc=1, device_id={"stat": lax.rem(me + k, stat_count)},
+                            device_id_type=pl.DeviceIdType.MESH)
+    for j in range(1, time_count):
+        pl.semaphore_signal(barrier, inc=1, device_id={"tm": lax.rem(now + j, time_count)},
+                            device_id_type=pl.DeviceIdType.MESH)
+    pl.semaphore_wait(barrier, stat_count + time_count - 2)
+
+    order = sorted(range(1, stat_count), key=lambda k: (-min(k, stat_count - k), k))
+    copies, wcopies = {}, {}
+    for k in order:
+        there = lax.rem(me + k, stat_count)
+        copies[k] = pltpu.make_async_remote_copy(
+            src_ref=spec_ref.at[there], dst_ref=place(now, me),
+            send_sem=send.at[k], recv_sem=recv.at[k],
+            device_id={"stat": there}, device_id_type=pl.DeviceIdType.MESH)
+        copies[k].start()
+    made = forward(me, spec_ref.at[me], 0)
+    take = pltpu.make_async_copy(spec_ref.at[me], own, loc)
+    wtake = pltpu.make_async_copy(w_ref, wown, wloc)
+    take.start()
+    wtake.start()
+    for k in order:
+        there = lax.rem(me + k, stat_count)
+        wcopies[k] = pltpu.make_async_remote_copy(
+            src_ref=w_ref, dst_ref=wg_ref.at[me],
+            send_sem=wsend.at[k], recv_sem=wrecv.at[k],
+            device_id={"stat": there}, device_id_type=pl.DeviceIdType.MESH)
+        wcopies[k].start()
+    take.wait()
+    wtake.wait()
+    put = pltpu.make_async_copy(own, place(now, me), loc)
+    wput = pltpu.make_async_copy(wown, wg_ref.at[me], wloc)
+    put.start()
+    wput.start()
+    for k in reversed(order):
+        copies[k].wait_recv()
+        source = lax.rem(me + stat_count - k, stat_count)
+        made += forward(source, place(now, source), k)
+    for k in order:
+        copies[k].wait_send()
+        wcopies[k].wait()
+    put.wait()
+    wput.wait()
+    for copy in made:
+        copy.wait()
+
+
+def exchange(blocks, weights, stat_count, time_count):
+    _, vch, depth, width = blocks.shape
+    dma = pltpu.SemaphoreType.DMA
+    peers = dma((stat_count,))
+    return pl.pallas_call(
+        functools.partial(exchange_kernel, stat_count, time_count),
+        in_specs=[pl.BlockSpec(memory_space=pl.ANY)] * 2,
+        out_specs=[pl.BlockSpec(memory_space=pl.ANY)] * 2,
+        out_shape=[
+            jax.ShapeDtypeStruct((vch, time_count, depth, stat_count * width), blocks.dtype),
+            jax.ShapeDtypeStruct((stat_count,) + weights.shape, weights.dtype),
+        ],
+        scratch_shapes=[
+            pltpu.VMEM(blocks.shape[1:], blocks.dtype), pltpu.VMEM(weights.shape, weights.dtype),
+            dma, dma, peers, peers, peers, peers,
+            dma((time_count, stat_count)), dma((time_count, stat_count)),
+        ],
+        compiler_params=pltpu.CompilerParams(collective_id=0, has_side_effects=True),
+        name="exchange",
+    )(blocks, weights)
+
+
+def correlate_kernel(scale, now_ref, y_ref, w_ref, beam_ref, vis_ref, cols, left):
+    now = now_ref[0]
+    _, times, depth, lanes = y_ref.shape
+    total = times * depth
+    half = 64
+    inputs = lanes // 2
+    mine = vis_ref.shape[2]
+    for time in range(times):
+        for tile in range(0, lanes, 256):
+            a = y_ref[0, time, :, tile:tile + 128]
+            b = y_ref[0, time, :, tile + 128:tile + 256]
+            out = pl.ds(tile // 2, 128)
+            cols[pl.ds(time * depth, depth), out] = jnp.concatenate([a[:, :half], b[:, :half]], 1)
+            cols[pl.ds(total + time * depth, depth), out] = jnp.concatenate([a[:, half:], b[:, half:]], 1)
+    for tile in range(0, mine, 128):
+        at = pl.ds(pl.multiple_of(now * mine + tile, 128), 128)
+        re = (cols[pl.ds(0, total), at]).T
+        im = (cols[pl.ds(total, total), at]).T
+        left[pl.ds(tile, 128), pl.ds(0, total)] = re
+        left[pl.ds(tile, 128), pl.ds(total, total)] = im
+        left[pl.ds(mine + tile, 128), pl.ds(0, total)] = im
+        left[pl.ds(mine + tile, 128), pl.ds(total, total)] = -re
+    block = 256
+
+    @pl.loop(0, inputs // block)
+    def _(n):
+        at = pl.ds(pl.multiple_of(n * block, block), block)
+        for q in range(2):
+            vis_ref[0, q, :, at] = scale * jnp.dot(
+                left[pl.ds(q * mine, mine), :], cols[:, at], preferred_element_type=jnp.float32)
+
+    beam_ref[0] = jnp.dot(
+        y_ref[0, now], w_ref[...], preferred_element_type=jnp.float32).astype(jnp.bfloat16)
+
+
+def correlate(spread, weights, now, scale, mine):
+    vch, times, depth, lanes = spread.shape
+    wide = weights.shape[1]
+    inputs = lanes // 2
+    return pl.pallas_call(
+        functools.partial(correlate_kernel, scale),
+        grid_spec=pltpu.PrefetchScalarGridSpec(
+            num_scalar_prefetch=1,
+            grid=(vch,),
+            in_specs=[
+                pl.BlockSpec((1, times, depth, lanes), lambda v, t: (v, 0, 0, 0)),
+                pl.BlockSpec(weights.shape, lambda v, t: (0, 0)),
+            ],
+            out_specs=[
+                pl.BlockSpec((1, depth, wide), lambda v, t: (v, 0, 0)),
+                pl.BlockSpec((1, 2, mine, inputs), lambda v, t: (v, 0, 0, 0)),
+            ],
+            scratch_shapes=[
+                pltpu.VMEM((2 * times * depth, inputs), jnp.bfloat16),
+                pltpu.VMEM((2 * mine, 2 * times * depth), jnp.bfloat16),
+            ],
+        ),
+        out_shape=[
+            jax.ShapeDtypeStruct((vch, depth, wide), jnp.bfloat16),
+            jax.ShapeDtypeStruct((vch, 2, mine, inputs), jnp.float32),
+        ],
+        name="correlate",
+    )(now, spread, weights)
+
+
+def fast_body(voltages, beam_weights):
+    stat_count = lax.axis_size("stat")
+    time_count = lax.axis_size("tm")
+    _, rows, items, points = voltages.shape
+    beams_count = beam_weights.shape[2]
+    local_vch = points // stat_count // AVG
+    fine = AVG // RADIX
+    width = 2 * rows
+    blocks = spectra_blocks(voltages, stat_count, local_vch)
+    blocks = blocks.reshape(stat_count, local_vch, items * AVG, width)
+    spread, gathered = exchange(blocks, beam_weights.reshape(width, beams_count), stat_count, time_count)
+    gathered = gathered.reshape(stat_count, 2, rows, beams_count)
+    w0, w1 = gathered[:, 0], gathered[:, 1]
+    stacked = jnp.stack([jnp.concatenate([w0, w1], 2), jnp.concatenate([-w1, w0], 2)], 1)
+    stacked = stacked.reshape(stat_count * width, 2 * beams_count)
+    now = lax.axis_index("tm").astype(jnp.int32).reshape(1)
+    scale = 1.0 / (items * time_count * AVG)
+    beams, vis = correlate(spread, stacked, now, scale, stat_count * rows // time_count)
+    beams = beams.reshape(local_vch, items, RADIX, fine, 2, beams_count).transpose(0, 3, 2, 1, 4, 5)
+    beams = beams.reshape(local_vch * AVG, items, 2, beams_count)
+    return beams, vis.transpose(2, 0, 1, 3)
+
+
+def fits_tiles(mesh, voltages):
+    _, inputs, spectra, points = voltages.shape
+    rows = inputs // mesh.shape["stat"]
+    mine = inputs // mesh.shape["tm"]
+    share = points // mesh.shape["stat"]
+    return 2 * rows == 128 and mine % 128 == 0 and share % AVG == 0 and spectra // mesh.shape["tm"] <= 4 and mesh.shape["tm"] <= 2
+
 
 def solution(mesh):
-    return jax.shard_map(
-        body,
-        mesh=mesh,
-        in_specs=(P(None, "stat", "tm", None), P(None, "stat", None)),
-        out_specs=(P("stat", "tm", None, None), P("tm", "stat", None, None)),
-        check_vma=False,
-    )
+    def whole(voltages, beam_weights):
+        return jax.shard_map(
+            fast_body if fits_tiles(mesh, voltages) else body,
+            mesh=mesh,
+            in_specs=(P(None, "stat", "tm", None), P(None, "stat", None)),
+            out_specs=(P("stat", "tm", None, None), P("tm", "stat", None, None)),
+            check_vma=False,
+        )(voltages, beam_weights)
+
+    return whole

time: 381 us -> 245 us (0.64)
  the two profiles are of different devices: /device:TPU:0 before, /device:TPU:11 now
where the time goes in v1:
time: 245 us
  Pallas kernels  215 us (88%)
  local copies, waits for them, and re-layouts  26.6 us (11%)
  other arithmetic  2.77 us (1%)
    pallas_call x1, Pallas kernels, exchange(): pl.pallas_call(functools.partial(exchange_kernel, stat_count, time_count)...  184 us
    unnamed x2, local copies, waits for them, and re-layouts  21.9 us
    pallas_call x1, Pallas kernels, correlate(): pl.pallas_call(functools.partial(correlate_kernel, scale), grid_spec=pltp...  20.2 us
    pallas_call x1, Pallas kernels, spectra_blocks(): pl.pallas_call(fft_kernel, grid=(items,), in_specs=[pl.BlockSpec((2, 1, r...  10.6 us

profile of v1, /device:TPU:11, one launch (start us, length us, event | category | flops | bytes accessed | tf_op | source)
XLA Modules:
  0.0 245.0 jit_solution(782335726528759119)
XLA Ops:
  0.6 6.5 %copy.16 = bf16[2,64,4,4096]{3,1,2,0:T(8,128)(2,1)} copy(bf16[2,64,4,4096]{3,2,1,0:T(4,128)(2,1)} %param.5) | data formatting | bytes 8388608 | tf_op args[0]
  7.1 10.6 %fft.1 = bf16[16,2,4,8,16,128]{5,4,3,2,1,0:T(8,128)(2,1)} custom-call(bf16[2,4,64,4096]{3,2,1,0:T(8,128)(2,1)} %bitcast.28, bf16[512,1024]{1,0:T(8,128)(2,1)} %constant.10.clone.m_ref, f32[8,512]{1,0:T(8,128)} %constant.11.clone.cos_ref, f32[8,512]{1,0:T(8,128)} %constant.12.clone.sin_ref), custom_call_target="tpu_custom_call" | custom-call | tf_op jit(solution)/shard_map/fft/pallas_call | solution.py:184
  17.7 184.2 %exchange.1 = (bf16[2,2,512,2048]{3,2,1,0:T(8,128)(2,1)}, bf16[16,128,256]{2,1,0:T(8,128)(2,1)}) custom-call(bf16[16,2,512,128]{3,2,1,0:T(8,128)(2,1)} %bitcast.27, bf16[128,256]{1,0:T(8,128)(2,1)} %bitcast.35), custom_call_target="tpu_custom_call" | custom-call | tf_op jit(solution)/shard_map/exchange/pallas_call | solution.py:276
  202.0 1.1 fusion
  203.1 1.3 slice_bitcast_fusion
  204.3 0.2 maximum_bitcast_fusion
  204.5 1.5 pad_maximum_fusion
  206.0 20.2 %correlate.1 = (bf16[2,512,512]{2,1,0:T(8,128)(2,1)}, f32[2,2,512,1024]{3,2,1,0:T(8,128)}) custom-call(s32[1]{0:T(128)} %bitcast.now_ref, bf16[2,2,512,2048]{3,2,1,0:T(8,128)(2,1)} %get-tuple-element.6.y_ref, bf16[2048,512]{1,0:T(8,128)(2,1)} %bitcast.30), custom_call_target="tpu_custom_call" | custom-call | tf_op jit(solution)/shard_map/correlate/pallas_call | solution.py:333
  226.3 1.3 reshape.30
  227.6 2.1 copy.11
  229.7 15.4 %copy.12 = f32[512,2,2,1024]{3,2,1,0:T(2,128)} copy(f32[512,2,2,1024]{3,0,2,1:T(8,128)} %bitcast.29) | data formatting | bytes 16777216

commit v2 on v1

--- a/solution.py
+++ b/solution.py
@@ -201,6 +201,21 @@
     )(voltages.transpose(0, 2, 1, 3), matrix, cos_turn, sin_turn)
 
 
+def send_order(count):
+    near = []
+    half = 1
+    while half < count // 4:
+        near += [(half, j) for j in range(half)]
+        half *= 2
+    far = [(count // 2, j) for j in range(count // 2)]
+    middle = [(half, j) for j in range(half)] if half < count // 2 else []
+    mixed = []
+    while far or middle:
+        mixed += far[:2] + middle[:1]
+        far, middle = far[2:], middle[1:]
+    return near + mixed
+
+
 def exchange_kernel(stat_count, time_count, spec_ref, w_ref, y_ref, wg_ref, own, wown, loc, wloc,
                     send, recv, wsend, wrecv, fsend, frecv):
     me, now = lax.axis_index("stat"), lax.axis_index("tm")
@@ -229,13 +244,19 @@
                             device_id_type=pl.DeviceIdType.MESH)
     pl.semaphore_wait(barrier, stat_count + time_count - 2)
 
-    order = sorted(range(1, stat_count), key=lambda k: (-min(k, stat_count - k), k))
+    order = send_order(stat_count)
+
+    def partner(k, sign):
+        half = k[0]
+        other = me // half + 1 - 2 * lax.rem(me // half, 2)
+        return other * half + lax.rem(lax.rem(me, half) + half + sign * k[1], half)
+
     copies, wcopies = {}, {}
-    for k in order:
-        there = lax.rem(me + k, stat_count)
+    for slot, k in enumerate(order, 1):
+        there = partner(k, 1)
         copies[k] = pltpu.make_async_remote_copy(
             src_ref=spec_ref.at[there], dst_ref=place(now, me),
-            send_sem=send.at[k], recv_sem=recv.at[k],
+            send_sem=send.at[slot], recv_sem=recv.at[slot],
             device_id={"stat": there}, device_id_type=pl.DeviceIdType.MESH)
         copies[k].start()
     made = forward(me, spec_ref.at[me], 0)
@@ -243,11 +264,11 @@
     wtake = pltpu.make_async_copy(w_ref, wown, wloc)
     take.start()
     wtake.start()
-    for k in order:
-        there = lax.rem(me + k, stat_count)
+    for slot, k in enumerate(order, 1):
+        there = partner(k, 1)
         wcopies[k] = pltpu.make_async_remote_copy(
             src_ref=w_ref, dst_ref=wg_ref.at[me],
-            send_sem=wsend.at[k], recv_sem=wrecv.at[k],
+            send_sem=wsend.at[slot], recv_sem=wrecv.at[slot],
             device_id={"stat": there}, device_id_type=pl.DeviceIdType.MESH)
         wcopies[k].start()
     take.wait()
@@ -256,10 +277,10 @@
     wput = pltpu.make_async_copy(wown, wg_ref.at[me], wloc)
     put.start()
     wput.start()
-    for k in reversed(order):
+    for slot, k in enumerate(order, 1):
         copies[k].wait_recv()
-        source = lax.rem(me + stat_count - k, stat_count)
-        made += forward(source, place(now, source), k)
+        source = partner(k, -1)
+        made += forward(source, place(now, source), slot)
     for k in order:
         copies[k].wait_send()
         wcopies[k].wait()
@@ -291,13 +312,17 @@
     )(blocks, weights)
 
 
-def correlate_kernel(scale, now_ref, y_ref, w_ref, beam_ref, vis_ref, cols, left):
+def correlate_kernel(scale, now_ref, y_ref, w_ref, beam_ref, vis_ref, cols, left, stacked):
     now = now_ref[0]
     _, times, depth, lanes = y_ref.shape
     total = times * depth
     half = 64
     inputs = lanes // 2
-    mine = vis_ref.shape[2]
+    mine = vis_ref.shape[0]
+    groups = vis_ref.shape[2]
+    flat = vis_ref.reshape(mine * groups, 128)
+    width, beams = w_ref.shape[1:]
+    rows = width // 2
     for time in range(times):
         for tile in range(0, lanes, 256):
             a = y_ref[0, time, :, tile:tile + 128]
@@ -319,16 +344,27 @@
     def _(n):
         at = pl.ds(pl.multiple_of(n * block, block), block)
         for q in range(2):
-            vis_ref[0, q, :, at] = scale * jnp.dot(
+            value = scale * jnp.dot(
                 left[pl.ds(q * mine, mine), :], cols[:, at], preferred_element_type=jnp.float32)
-
+            for part in range(block // 128):
+                row = (n * (block // 128) + part) * 2 + q
+                flat[pl.ds(row, mine, stride=groups), :] = value[:, part * 128:part * 128 + 128]
+
+    for source in range(w_ref.shape[0]):
+        upper = pl.ds(source * width, rows)
+        lower = pl.ds(source * width + rows, rows)
+        stacked[upper, pl.ds(0, beams)] = w_ref[source, :rows]
+        stacked[upper, pl.ds(beams, beams)] = w_ref[source, rows:]
+        stacked[lower, pl.ds(0, beams)] = -w_ref[source, rows:]
+        stacked[lower, pl.ds(beams, beams)] = w_ref[source, :rows]
     beam_ref[0] = jnp.dot(
-        y_ref[0, now], w_ref[...], preferred_element_type=jnp.float32).astype(jnp.bfloat16)
+        y_ref[0, now], stacked[...], preferred_element_type=jnp.float32).astype(jnp.bfloat16)
 
 
 def correlate(spread, weights, now, scale, mine):
     vch, times, depth, lanes = spread.shape
-    wide = weights.shape[1]
+    wide = 2 * weights.shape[2]
+    groups = lanes // 128
     inputs = lanes // 2
     return pl.pallas_call(
         functools.partial(correlate_kernel, scale),
@@ -337,20 +373,21 @@
             grid=(vch,),
             in_specs=[
                 pl.BlockSpec((1, times, depth, lanes), lambda v, t: (v, 0, 0, 0)),
-                pl.BlockSpec(weights.shape, lambda v, t: (0, 0)),
+                pl.BlockSpec(weights.shape, lambda v, t: (0, 0, 0)),
             ],
             out_specs=[
                 pl.BlockSpec((1, depth, wide), lambda v, t: (v, 0, 0)),
-                pl.BlockSpec((1, 2, mine, inputs), lambda v, t: (v, 0, 0, 0)),
+                pl.BlockSpec((mine, 1, groups, 128), lambda v, t: (0, v, 0, 0)),
             ],
             scratch_shapes=[
                 pltpu.VMEM((2 * times * depth, inputs), jnp.bfloat16),
                 pltpu.VMEM((2 * mine, 2 * times * depth), jnp.bfloat16),
+                pltpu.VMEM((lanes, wide), jnp.bfloat16),
             ],
         ),
         out_shape=[
             jax.ShapeDtypeStruct((vch, depth, wide), jnp.bfloat16),
-            jax.ShapeDtypeStruct((vch, 2, mine, inputs), jnp.float32),
+            jax.ShapeDtypeStruct((mine, vch, groups, 128), jnp.float32),
         ],
         name="correlate",
     )(now, spread, weights)
@@ -367,16 +404,13 @@
     blocks = spectra_blocks(voltages, stat_count, local_vch)
     blocks = blocks.reshape(stat_count, local_vch, items * AVG, width)
     spread, gathered = exchange(blocks, beam_weights.reshape(width, beams_count), stat_count, time_count)
-    gathered = gathered.reshape(stat_count, 2, rows, beams_count)
-    w0, w1 = gathered[:, 0], gathered[:, 1]
-    stacked = jnp.stack([jnp.concatenate([w0, w1], 2), jnp.concatenate([-w1, w0], 2)], 1)
-    stacked = stacked.reshape(stat_count * width, 2 * beams_count)
     now = lax.axis_index("tm").astype(jnp.int32).reshape(1)
     scale = 1.0 / (items * time_count * AVG)
-    beams, vis = correlate(spread, stacked, now, scale, stat_count * rows // time_count)
+    beams, vis = correlate(spread, gathered, now, scale, stat_count * rows // time_count)
     beams = beams.reshape(local_vch, items, RADIX, fine, 2, beams_count).transpose(0, 3, 2, 1, 4, 5)
     beams = beams.reshape(local_vch * AVG, items, 2, beams_count)
-    return beams, vis.transpose(2, 0, 1, 3)
+    vis = vis.reshape(vis.shape[0], local_vch, -1, 2, 128).transpose(0, 1, 3, 2, 4)
+    return beams, vis.reshape(vis.shape[0], local_vch, 2, stat_count * rows)
 
 
 def fits_tiles(mesh, voltages):
@@ -384,7 +418,8 @@
     rows = inputs // mesh.shape["stat"]
     mine = inputs // mesh.shape["tm"]
     share = points // mesh.shape["stat"]
-    return 2 * rows == 128 and mine % 128 == 0 and share % AVG == 0 and spectra // mesh.shape["tm"] <= 4 and mesh.shape["tm"] <= 2
+    even = mesh.shape["stat"] & (mesh.shape["stat"] - 1) == 0 and mesh.shape["stat"] >= 4
+    return even and 2 * rows == 128 and mine % 128 == 0 and share % AVG == 0 and spectra // mesh.shape["tm"] <= 4 and mesh.shape["tm"] <= 2
 
 
 def solution(mesh):

time: 245 us -> 176 us (0.72)
  the two profiles are of different devices: /device:TPU:11 before, /device:TPU:0 now
where the time goes in v2:
time: 176 us; the launch traced here: 174 us
  Pallas kernels  163 us (93%)
  local copies, waits for them, and re-layouts  9.92 us (6%)
    pallas_call x1, Pallas kernels, exchange(): pl.pallas_call(functools.partial(exchange_kernel, stat_count, time_count)...  130 us
    pallas_call x1, Pallas kernels, correlate(): pl.pallas_call(functools.partial(correlate_kernel, scale), grid_spec=pltp...  22.6 us
    pallas_call x1, Pallas kernels, spectra_blocks(): pl.pallas_call(fft_kernel, grid=(items,), in_specs=[pl.BlockSpec((2, 1, r...  10.6 us
    unnamed x1, local copies, waits for them, and re-layouts  6.5 us

profile of v2, /device:TPU:0, one launch (start us, length us, event | category | flops | bytes accessed | tf_op | source)
XLA Modules:
  0.0 173.9 jit_solution(14944371374375887556)
XLA Ops:
  0.6 6.5 %copy.11 = bf16[2,64,4,4096]{3,1,2,0:T(8,128)(2,1)} copy(bf16[2,64,4,4096]{3,2,1,0:T(4,128)(2,1)} %param.5) | data formatting | bytes 8388608 | tf_op args[0]
  7.1 10.6 %fft.1 = bf16[16,2,4,8,16,128]{5,4,3,2,1,0:T(8,128)(2,1)} custom-call(bf16[2,4,64,4096]{3,2,1,0:T(8,128)(2,1)} %bitcast.14, bf16[512,1024]{1,0:T(8,128)(2,1)} %constant.10.clone.m_ref, f32[8,512]{1,0:T(8,128)} %constant.11.clone.cos_ref, f32[8,512]{1,0:T(8,128)} %constant.12.clone.sin_ref), custom_call_target="tpu_custom_call" | custom-call | tf_op jit(solution)/shard_map/fft/pallas_call | solution.py:184
  17.8 130.1 %exchange.1 = (bf16[2,2,512,2048]{3,2,1,0:T(8,128)(2,1)}, bf16[16,128,256]{2,1,0:T(8,128)(2,1)}) custom-call(bf16[16,2,512,128]{3,2,1,0:T(8,128)(2,1)} %bitcast.13, bf16[128,256]{1,0:T(8,128)(2,1)} %bitcast.17), custom_call_target="tpu_custom_call" | custom-call | tf_op jit(solution)/shard_map/exchange/pallas_call | solution.py:297
  147.9 22.6 %correlate.1 = (bf16[2,512,512]{2,1,0:T(8,128)(2,1)}, f32[512,2,16,128]{3,2,1,0:T(8,128)}) custom-call(s32[1]{0:T(128)} %bitcast.now_ref, bf16[2,2,512,2048]{3,2,1,0:T(8,128)(2,1)} %get-tuple-element.6.y_ref, bf16[16,128,256]{2,1,0:T(8,128)(2,1)} %get-tuple-element.7.w_ref), custom_call_target="tpu_custom_call" | custom-call | tf_op jit(solution)/shard_map/correlate/pallas_call | solution.py:369
  170.5 1.3 reshape.28
  171.9 2.1 %copy.8 = bf16[2,16,8,4,2,256]{5,4,3,2,1,0:T(2,128)(2,1)} copy(bf16[2,16,8,4,2,256]{5,4,1,2,3,0:T(2,128)(2,1)S(1)} %bitcast.15) | data formatting | bytes 2097152 | tf_op jit(solution)/shard_map/transpose | solution.py:410

commit v3 on v2

--- a/solution.py
+++ b/solution.py
@@ -201,28 +201,12 @@
     )(voltages.transpose(0, 2, 1, 3), matrix, cos_turn, sin_turn)
 
 
-def send_order(count):
-    near = []
-    half = 1
-    while half < count // 4:
-        near += [(half, j) for j in range(half)]
-        half *= 2
-    far = [(count // 2, j) for j in range(count // 2)]
-    middle = [(half, j) for j in range(half)] if half < count // 2 else []
-    mixed = []
-    while far or middle:
-        mixed += far[:2] + middle[:1]
-        far, middle = far[2:], middle[1:]
-    return near + mixed
-
-
 def exchange_kernel(stat_count, time_count, spec_ref, w_ref, y_ref, wg_ref, own, wown, loc, wloc,
                     send, recv, wsend, wrecv, fsend, frecv):
     me, now = lax.axis_index("stat"), lax.axis_index("tm")
-    width = spec_ref.shape[-1]
 
     def place(time, source):
-        return y_ref.at[:, time, :, pl.ds(pl.multiple_of(source * width, width), width)]
+        return y_ref.at[time, source]
 
     def forward(source, src, k):
         made = []
@@ -244,46 +228,60 @@
                             device_id_type=pl.DeviceIdType.MESH)
     pl.semaphore_wait(barrier, stat_count + time_count - 2)
 
-    order = send_order(stat_count)
-
-    def partner(k, sign):
-        half = k[0]
-        other = me // half + 1 - 2 * lax.rem(me // half, 2)
-        return other * half + lax.rem(lax.rem(me, half) + half + sign * k[1], half)
-
-    copies, wcopies = {}, {}
-    for slot, k in enumerate(order, 1):
-        there = partner(k, 1)
-        copies[k] = pltpu.make_async_remote_copy(
-            src_ref=spec_ref.at[there], dst_ref=place(now, me),
-            send_sem=send.at[slot], recv_sem=recv.at[slot],
+    half, quarter = stat_count // 2, stat_count // 4
+    upper = me // half
+    spot = lax.rem(me, quarter)
+    inner = lax.rem(me // quarter + upper, 2)
+
+    def turned(base, sign, r):
+        return base + lax.rem(spot + quarter + sign * r, quarter)
+
+    bases = ((1 - upper) * half + upper * quarter, (1 - upper) * (half + quarter))
+    beside = (2 * upper + 1 - lax.rem(me // quarter, 2)) * quarter
+    own_quarter = me // quarter * quarter
+    sends, sources = [], []
+    for r in range(1, quarter):
+        sends.append((turned(own_quarter, 1, r), r))
+        sources.append((turned(own_quarter, -1, r), r))
+    for r in range(quarter):
+        for place_of in range(2):
+            sends.append((turned(bases[place_of], 1, r), 2 * quarter + (1 - inner) * quarter + r))
+        sends.append((turned(beside, 1, r), quarter + r))
+        sources.append((turned(beside, -1, r), quarter + r))
+        sources.append((turned(bases[0], -1, r), 2 * quarter + r))
+    for r in range(quarter):
+        sources.append((turned(bases[1], -1, r), 3 * quarter + r))
+
+    def to(src, dst, there, out_sem, in_sem):
+        return pltpu.make_async_remote_copy(
+            src_ref=src, dst_ref=dst, send_sem=out_sem, recv_sem=in_sem,
             device_id={"stat": there}, device_id_type=pl.DeviceIdType.MESH)
-        copies[k].start()
+
+    copies, wcopies = [], []
+    for number, (there, slot) in enumerate(sends):
+        copies.append(to(spec_ref.at[there], place(now, me), there, send.at[number], recv.at[slot]))
+        copies[-1].start()
     made = forward(me, spec_ref.at[me], 0)
     take = pltpu.make_async_copy(spec_ref.at[me], own, loc)
     wtake = pltpu.make_async_copy(w_ref, wown, wloc)
     take.start()
     wtake.start()
-    for slot, k in enumerate(order, 1):
-        there = partner(k, 1)
-        wcopies[k] = pltpu.make_async_remote_copy(
-            src_ref=w_ref, dst_ref=wg_ref.at[me],
-            send_sem=wsend.at[slot], recv_sem=wrecv.at[slot],
-            device_id={"stat": there}, device_id_type=pl.DeviceIdType.MESH)
-        wcopies[k].start()
+    for number, (there, slot) in enumerate(sends):
+        wcopies.append(to(w_ref, wg_ref.at[me], there, wsend.at[number], wrecv.at[slot]))
+        wcopies[-1].start()
     take.wait()
     wtake.wait()
     put = pltpu.make_async_copy(own, place(now, me), loc)
     wput = pltpu.make_async_copy(wown, wg_ref.at[me], wloc)
     put.start()
     wput.start()
-    for slot, k in enumerate(order, 1):
-        copies[k].wait_recv()
-        source = partner(k, -1)
+    for source, slot in sources:
+        to(spec_ref.at[source], place(now, source), source, send.at[0], recv.at[slot]).wait_recv()
         made += forward(source, place(now, source), slot)
-    for k in order:
-        copies[k].wait_send()
-        wcopies[k].wait()
+    for source, slot in sources:
+        to(w_ref, wg_ref.at[source], source, wsend.at[0], wrecv.at[slot]).wait_recv()
+    for copy in copies + wcopies:
+        copy.wait_send()
     put.wait()
     wput.wait()
     for copy in made:
@@ -291,7 +289,6 @@
 
 
 def exchange(blocks, weights, stat_count, time_count):
-    _, vch, depth, width = blocks.shape
     dma = pltpu.SemaphoreType.DMA
     peers = dma((stat_count,))
     return pl.pallas_call(
@@ -299,7 +296,7 @@
         in_specs=[pl.BlockSpec(memory_space=pl.ANY)] * 2,
         out_specs=[pl.BlockSpec(memory_space=pl.ANY)] * 2,
         out_shape=[
-            jax.ShapeDtypeStruct((vch, time_count, depth, stat_count * width), blocks.dtype),
+            jax.ShapeDtypeStruct((time_count,) + blocks.shape, blocks.dtype),
             jax.ShapeDtypeStruct((stat_count,) + weights.shape, weights.dtype),
         ],
         scratch_shapes=[
@@ -314,20 +311,19 @@
 
 def correlate_kernel(scale, now_ref, y_ref, w_ref, beam_ref, vis_ref, cols, left, stacked):
     now = now_ref[0]
-    _, times, depth, lanes = y_ref.shape
+    times, sources, _, depth, width = y_ref.shape
     total = times * depth
-    half = 64
-    inputs = lanes // 2
+    half = width // 2
+    inputs = sources * half
     mine = vis_ref.shape[0]
     groups = vis_ref.shape[2]
     flat = vis_ref.reshape(mine * groups, 128)
-    width, beams = w_ref.shape[1:]
-    rows = width // 2
+    beams = w_ref.shape[2]
     for time in range(times):
-        for tile in range(0, lanes, 256):
-            a = y_ref[0, time, :, tile:tile + 128]
-            b = y_ref[0, time, :, tile + 128:tile + 256]
-            out = pl.ds(tile // 2, 128)
+        for source in range(0, sources, 2):
+            a = y_ref[time, source, 0]
+            b = y_ref[time, source + 1, 0]
+            out = pl.ds(source * half, width)
             cols[pl.ds(time * depth, depth), out] = jnp.concatenate([a[:, :half], b[:, :half]], 1)
             cols[pl.ds(total + time * depth, depth), out] = jnp.concatenate([a[:, half:], b[:, half:]], 1)
     for tile in range(0, mine, 128):
@@ -350,19 +346,25 @@
                 row = (n * (block // 128) + part) * 2 + q
                 flat[pl.ds(row, mine, stride=groups), :] = value[:, part * 128:part * 128 + 128]
 
-    for source in range(w_ref.shape[0]):
-        upper = pl.ds(source * width, rows)
-        lower = pl.ds(source * width + rows, rows)
-        stacked[upper, pl.ds(0, beams)] = w_ref[source, :rows]
-        stacked[upper, pl.ds(beams, beams)] = w_ref[source, rows:]
-        stacked[lower, pl.ds(0, beams)] = -w_ref[source, rows:]
-        stacked[lower, pl.ds(beams, beams)] = w_ref[source, :rows]
-    beam_ref[0] = jnp.dot(
-        y_ref[0, now], stacked[...], preferred_element_type=jnp.float32).astype(jnp.bfloat16)
+    for source in range(sources):
+        upper = pl.ds(source * half, half)
+        lower = pl.ds(inputs + source * half, half)
+        stacked[upper, pl.ds(0, beams)] = w_ref[source, :half]
+        stacked[upper, pl.ds(beams, beams)] = w_ref[source, half:]
+        stacked[lower, pl.ds(0, beams)] = -w_ref[source, half:]
+        stacked[lower, pl.ds(beams, beams)] = w_ref[source, :half]
+    shift = pl.multiple_of(now * depth, depth)
+    real = jnp.dot(
+        cols[pl.ds(shift, depth), :], stacked[pl.ds(0, inputs), :], preferred_element_type=jnp.float32)
+    imag = jnp.dot(
+        cols[pl.ds(total + shift, depth), :], stacked[pl.ds(inputs, inputs), :],
+        preferred_element_type=jnp.float32)
+    beam_ref[0] = (real + imag).astype(jnp.bfloat16)
 
 
 def correlate(spread, weights, now, scale, mine):
-    vch, times, depth, lanes = spread.shape
+    times, sources, vch, depth, width = spread.shape
+    lanes = sources * width
     wide = 2 * weights.shape[2]
     groups = lanes // 128
     inputs = lanes // 2
@@ -372,7 +374,7 @@
             num_scalar_prefetch=1,
             grid=(vch,),
             in_specs=[
-                pl.BlockSpec((1, times, depth, lanes), lambda v, t: (v, 0, 0, 0)),
+                pl.BlockSpec((times, sources, 1, depth, width), lambda v, t: (0, 0, v, 0, 0)),
                 pl.BlockSpec(weights.shape, lambda v, t: (0, 0, 0)),
             ],
             out_specs=[

time: 176 us -> 185 us (1.051); the launches traced: 174 us -> 185 us
  Pallas kernels: 163 us -> 174 us
    pallas_call x1, Pallas kernels: 130 us -> 141 us  [exchange(): pl.pallas_call(functools.partial(exchange_kernel, stat_count, time_count)...]
where the time goes in v3:
time: 185 us
  Pallas kernels  174 us (94%)
  local copies, waits for them, and re-layouts  9.92 us (5%)
    pallas_call x1, Pallas kernels, exchange(): pl.pallas_call(functools.partial(exchange_kernel, stat_count, time_count)...  141 us
    pallas_call x1, Pallas kernels, correlate(): pl.pallas_call(functools.partial(correlate_kernel, scale), grid_spec=pltp...  22.7 us
    pallas_call x1, Pallas kernels, spectra_blocks(): pl.pallas_call(fft_kernel, grid=(items,), in_specs=[pl.BlockSpec((2, 1, r...  10.6 us
    unnamed x1, local copies, waits for them, and re-layouts  6.5 us

profile of v3, /device:TPU:0, one launch (start us, length us, event | category | flops | bytes accessed | tf_op | source)
XLA Modules:
  0.0 185.0 jit_solution(9433867793895663389)
XLA Ops:
  0.6 6.5 %copy.11 = bf16[2,64,4,4096]{3,1,2,0:T(8,128)(2,1)} copy(bf16[2,64,4,4096]{3,2,1,0:T(4,128)(2,1)} %param.5) | data formatting | bytes 8388608 | tf_op args[0]
  7.1 10.6 %fft.1 = bf16[16,2,4,8,16,128]{5,4,3,2,1,0:T(8,128)(2,1)} custom-call(bf16[2,4,64,4096]{3,2,1,0:T(8,128)(2,1)} %bitcast.14, bf16[512,1024]{1,0:T(8,128)(2,1)} %constant.10.clone.m_ref, f32[8,512]{1,0:T(8,128)} %constant.11.clone.cos_ref, f32[8,512]{1,0:T(8,128)} %constant.12.clone.sin_ref), custom_call_target="tpu_custom_call" | custom-call | tf_op jit(solution)/shard_map/fft/pallas_call | solution.py:184
  17.8 141.1 %exchange.1 = (bf16[2,16,2,512,128]{4,3,2,1,0:T(8,128)(2,1)}, bf16[16,128,256]{2,1,0:T(8,128)(2,1)}) custom-call(bf16[16,2,512,128]{3,2,1,0:T(8,128)(2,1)} %bitcast.13, bf16[128,256]{1,0:T(8,128)(2,1)} %bitcast.17), custom_call_target="tpu_custom_call" | custom-call | tf_op jit(solution)/shard_map/exchange/pallas_call | solution.py:294
  158.9 22.7 %correlate.1 = (bf16[2,512,512]{2,1,0:T(8,128)(2,1)}, f32[512,2,16,128]{3,2,1,0:T(8,128)}) custom-call(s32[1]{0:T(128)} %bitcast.now_ref, bf16[2,16,2,512,128]{4,3,2,1,0:T(8,128)(2,1)} %get-tuple-element.6.y_ref, bf16[16,128,256]{2,1,0:T(8,128)(2,1)} %get-tuple-element.7.w_ref), custom_call_target="tpu_custom_call" | custom-call | tf_op jit(solution)/shard_map/correlate/pallas_call | solution.py:371
  181.6 1.3 reshape.28
  182.9 2.1 %copy.8 = bf16[2,16,8,4,2,256]{5,4,3,2,1,0:T(2,128)(2,1)} copy(bf16[2,16,8,4,2,256]{5,4,1,2,3,0:T(2,128)(2,1)S(1)} %bitcast.15) | data formatting | bytes 2097152 | tf_op jit(solution)/shard_map/transpose | solution.py:412

commit v4 on v3

--- a/solution.py
+++ b/solution.py
@@ -201,6 +201,21 @@
     )(voltages.transpose(0, 2, 1, 3), matrix, cos_turn, sin_turn)
 
 
+def send_order(count):
+    near = []
+    half = 1
+    while half < count // 4:
+        near += [(half, j) for j in range(half)]
+        half *= 2
+    far = [(count // 2, j) for j in range(count // 2)]
+    middle = [(half, j) for j in range(half)] if half < count // 2 else []
+    mixed = []
+    while far or middle:
+        mixed += far[:2] + middle[:1]
+        far, middle = far[2:], middle[1:]
+    return near + mixed
+
+
 def exchange_kernel(stat_count, time_count, spec_ref, w_ref, y_ref, wg_ref, own, wown, loc, wloc,
                     send, recv, wsend, wrecv, fsend, frecv):
     me, now = lax.axis_index("stat"), lax.axis_index("tm")
@@ -208,12 +223,14 @@
     def place(time, source):
         return y_ref.at[time, source]
 
-    def forward(source, src, k):
+    pieces = spec_ref.shape[1]
+
+    def forward(source, src, k, part):
         made = []
         for j in range(1, time_count):
             copy = pltpu.make_async_remote_copy(
-                src_ref=src, dst_ref=place(now, source),
-                send_sem=fsend.at[j, k], recv_sem=frecv.at[j, k],
+                src_ref=src.at[part], dst_ref=place(now, source).at[part],
+                send_sem=fsend.at[j, k * pieces + part], recv_sem=frecv.at[j, k * pieces + part],
                 device_id={"tm": lax.rem(now + j, time_count)}, device_id_type=pl.DeviceIdType.MESH)
             copy.start()
             made.append(copy)
@@ -228,62 +245,93 @@
                             device_id_type=pl.DeviceIdType.MESH)
     pl.semaphore_wait(barrier, stat_count + time_count - 2)
 
-    half, quarter = stat_count // 2, stat_count // 4
-    upper = me // half
-    spot = lax.rem(me, quarter)
-    inner = lax.rem(me // quarter + upper, 2)
-
-    def turned(base, sign, r):
-        return base + lax.rem(spot + quarter + sign * r, quarter)
-
-    bases = ((1 - upper) * half + upper * quarter, (1 - upper) * (half + quarter))
-    beside = (2 * upper + 1 - lax.rem(me // quarter, 2)) * quarter
-    own_quarter = me // quarter * quarter
-    sends, sources = [], []
-    for r in range(1, quarter):
-        sends.append((turned(own_quarter, 1, r), r))
-        sources.append((turned(own_quarter, -1, r), r))
-    for r in range(quarter):
-        for place_of in range(2):
-            sends.append((turned(bases[place_of], 1, r), 2 * quarter + (1 - inner) * quarter + r))
-        sends.append((turned(beside, 1, r), quarter + r))
-        sources.append((turned(beside, -1, r), quarter + r))
-        sources.append((turned(bases[0], -1, r), 2 * quarter + r))
-    for r in range(quarter):
-        sources.append((turned(bases[1], -1, r), 3 * quarter + r))
+    order = send_order(stat_count)
+
+    def partner(k, sign):
+        half = k[0]
+        other = me // half + 1 - 2 * lax.rem(me // half, 2)
+        return other * half + lax.rem(lax.rem(me, half) + half + sign * k[1], half)
+
+    sends = [(partner(k, 1), slot) for slot, k in enumerate(order, 1)]
+    sources = [(partner(k, -1), slot) for slot, k in enumerate(order, 1)]
 
     def to(src, dst, there, out_sem, in_sem):
         return pltpu.make_async_remote_copy(
             src_ref=src, dst_ref=dst, send_sem=out_sem, recv_sem=in_sem,
             device_id={"stat": there}, device_id_type=pl.DeviceIdType.MESH)
 
-    copies, wcopies = [], []
+    levels = []
+    reach = stat_count // 2
+    while reach:
+        levels.append(reach)
+        reach //= 2
+
+    def level_copies(level):
+        reach = levels[level]
+        period = 2 * reach
+        other = partner((reach, 0), 1)
+        made = []
+        for turn in range(stat_count // period):
+            block = lax.rem(me, period) + period * turn
+            index = stat_count // period + turn
+            made.append(to(
+                wg_ref.at[block] if level else w_ref, wg_ref.at[block], other,
+                wsend.at[index], wrecv.at[index]))
+        return made
+
+    def start_level(level):
+        started.append(level_copies(level))
+        for copy in started[-1]:
+            copy.start()
+
+    def end_level(level):
+        for copy in started[level]:
+            copy.wait_recv()
+
+    copies, started = [], []
+    wtake = pltpu.make_async_copy(w_ref, wown, wloc)
+    wtake.start()
+    start_level(0)
+    wtake.wait()
+    wput = pltpu.make_async_copy(wown, wg_ref.at[me], wloc)
+    wput.start()
+    early = 5
     for number, (there, slot) in enumerate(sends):
-        copies.append(to(spec_ref.at[there], place(now, me), there, send.at[number], recv.at[slot]))
-        copies[-1].start()
-    made = forward(me, spec_ref.at[me], 0)
+        if number == early:
+            wput.wait()
+            end_level(0)
+            start_level(1)
+        for part in range(pieces):
+            copies.append(to(
+                spec_ref.at[there, part], place(now, me).at[part], there,
+                send.at[number * pieces + part], recv.at[slot * pieces + part]))
+            copies[-1].start()
+    made = []
+    for part in range(pieces):
+        made += forward(me, spec_ref.at[me], 0, part)
     take = pltpu.make_async_copy(spec_ref.at[me], own, loc)
-    wtake = pltpu.make_async_copy(w_ref, wown, wloc)
     take.start()
-    wtake.start()
-    for number, (there, slot) in enumerate(sends):
-        wcopies.append(to(w_ref, wg_ref.at[me], there, wsend.at[number], wrecv.at[slot]))
-        wcopies[-1].start()
     take.wait()
-    wtake.wait()
     put = pltpu.make_async_copy(own, place(now, me), loc)
-    wput = pltpu.make_async_copy(wown, wg_ref.at[me], wloc)
     put.start()
-    wput.start()
-    for source, slot in sources:
-        to(spec_ref.at[source], place(now, source), source, send.at[0], recv.at[slot]).wait_recv()
-        made += forward(source, place(now, source), slot)
-    for source, slot in sources:
-        to(w_ref, wg_ref.at[source], source, wsend.at[0], wrecv.at[slot]).wait_recv()
-    for copy in copies + wcopies:
+    for number, (source, slot) in enumerate(sources):
+        if number % 4 == 3 and len(started) < len(levels):
+            end_level(len(started) - 1)
+            start_level(len(started))
+        for part in range(pieces):
+            to(spec_ref.at[source, part], place(now, source).at[part], source,
+               send.at[0], recv.at[slot * pieces + part]).wait_recv()
+            made += forward(source, place(now, source), slot, part)
+    while len(started) < len(levels):
+        end_level(len(started) - 1)
+        start_level(len(started))
+    end_level(len(levels) - 1)
+    for copy in copies:
         copy.wait_send()
+    for level in started:
+        for copy in level:
+            copy.wait_send()
     put.wait()
-    wput.wait()
     for copy in made:
         copy.wait()
 
@@ -291,6 +339,7 @@
 def exchange(blocks, weights, stat_count, time_count):
     dma = pltpu.SemaphoreType.DMA
     peers = dma((stat_count,))
+    parts = stat_count * blocks.shape[1]
     return pl.pallas_call(
         functools.partial(exchange_kernel, stat_count, time_count),
         in_specs=[pl.BlockSpec(memory_space=pl.ANY)] * 2,
@@ -301,8 +350,8 @@
         ],
         scratch_shapes=[
             pltpu.VMEM(blocks.shape[1:], blocks.dtype), pltpu.VMEM(weights.shape, weights.dtype),
-            dma, dma, peers, peers, peers, peers,
-            dma((time_count, stat_count)), dma((time_count, stat_count)),
+            dma, dma, dma((parts,)), dma((parts,)), peers, peers,
+            dma((time_count, parts)), dma((time_count, parts)),
         ],
         compiler_params=pltpu.CompilerParams(collective_id=0, has_side_effects=True),
         name="exchange",
@@ -420,7 +469,7 @@
     rows = inputs // mesh.shape["stat"]
     mine = inputs // mesh.shape["tm"]
     share = points // mesh.shape["stat"]
-    even = mesh.shape["stat"] & (mesh.shape["stat"] - 1) == 0 and mesh.shape["stat"] >= 4
+    even = mesh.shape["stat"] & (mesh.shape["stat"] - 1) == 0 and mesh.shape["stat"] >= 8
     return even and 2 * rows == 128 and mine % 128 == 0 and share % AVG == 0 and spectra // mesh.shape["tm"] <= 4 and mesh.shape["tm"] <= 2
 
 

time: 185 us -> 168 us (0.908)
  the two profiles are of different devices: /device:TPU:0 before, /device:TPU:9 now
where the time goes in v4:
time: 168 us; the launch traced here: 167 us
  Pallas kernels  157 us (93%)
  local copies, waits for them, and re-layouts  9.92 us (6%)
    pallas_call x1, Pallas kernels, exchange(): pl.pallas_call(functools.partial(exchange_kernel, stat_count, time_count)...  123 us
    pallas_call x1, Pallas kernels, correlate(): pl.pallas_call(functools.partial(correlate_kernel, scale), grid_spec=pltp...  22.7 us
    pallas_call x1, Pallas kernels, spectra_blocks(): pl.pallas_call(fft_kernel, grid=(items,), in_specs=[pl.BlockSpec((2, 1, r...  10.6 us
    unnamed x1, local copies, waits for them, and re-layouts  6.5 us

profile of v4, /device:TPU:9, one launch (start us, length us, event | category | flops | bytes accessed | tf_op | source)
XLA Modules:
  0.0 167.3 jit_solution(1899857787066241974)
XLA Ops:
  0.6 6.5 %copy.11 = bf16[2,64,4,4096]{3,1,2,0:T(8,128)(2,1)} copy(bf16[2,64,4,4096]{3,2,1,0:T(4,128)(2,1)} %param.5) | data formatting | bytes 8388608 | tf_op args[0]
  7.1 10.6 %fft.1 = bf16[16,2,4,8,16,128]{5,4,3,2,1,0:T(8,128)(2,1)} custom-call(bf16[2,4,64,4096]{3,2,1,0:T(8,128)(2,1)} %bitcast.14, bf16[512,1024]{1,0:T(8,128)(2,1)} %constant.10.clone.m_ref, f32[8,512]{1,0:T(8,128)} %constant.11.clone.cos_ref, f32[8,512]{1,0:T(8,128)} %constant.12.clone.sin_ref), custom_call_target="tpu_custom_call" | custom-call | tf_op jit(solution)/shard_map/fft/pallas_call | solution.py:184
  17.8 123.3 %exchange.1 = (bf16[2,16,2,512,128]{4,3,2,1,0:T(8,128)(2,1)}, bf16[16,128,256]{2,1,0:T(8,128)(2,1)}) custom-call(bf16[16,2,512,128]{3,2,1,0:T(8,128)(2,1)} %bitcast.13, bf16[128,256]{1,0:T(8,128)(2,1)} %bitcast.17), custom_call_target="tpu_custom_call" | custom-call | tf_op jit(solution)/shard_map/exchange/pallas_call | solution.py:343
  141.1 22.7 %correlate.1 = (bf16[2,512,512]{2,1,0:T(8,128)(2,1)}, f32[512,2,16,128]{3,2,1,0:T(8,128)}) custom-call(s32[1]{0:T(128)} %bitcast.now_ref, bf16[2,16,2,512,128]{4,3,2,1,0:T(8,128)(2,1)} %get-tuple-element.6.y_ref, bf16[16,128,256]{2,1,0:T(8,128)(2,1)} %get-tuple-element.7.w_ref), custom_call_target="tpu_custom_call" | custom-call | tf_op jit(solution)/shard_map/correlate/pallas_call | solution.py:420
  163.8 1.3 reshape.28
  165.2 2.1 %copy.8 = bf16[2,16,8,4,2,256]{5,4,3,2,1,0:T(2,128)(2,1)} copy(bf16[2,16,8,4,2,256]{5,4,1,2,3,0:T(2,128)(2,1)S(1)} %bitcast.15) | data formatting | bytes 2097152 | tf_op jit(solution)/shard_map/transpose | solution.py:461
